TPU v7x, 256 devices: a whole 4x4x8 slice. The times are simulated.
256 devices in a mesh: dp: 8 (over x, core), seq: 32 (over z, y).
Axes of the slice: x: 4, y: 4, z: 8, core: 2. Of those that a mesh axis runs over, the one named last changes fastest.
Arguments:
- layer_input: bfloat16 [8, 4096, 4096], P('dp', 'seq'), may hold values from -6 to 6
- proj_weight: bfloat16 [4096, 256], replicated, may hold values from -0.0078125 to 0.0078125
- inputs: bfloat16 [8, 4096, 2048], P('dp', 'seq'), may hold values from -6 to 6
- step_size: float32 [8, 32, 4096], P('dp', None, 'seq'), may hold values from 0.02 to 0.2
- log_decay: float32 [8, 32, 4096], P('dp', None, 'seq'), may hold values from -0.8 to 0, as said below
- skip_gain: float32 [32], replicated, may hold values from 0.1 to 1.9
- grad_out: bfloat16 [8, 4096, 2048], P('dp', 'seq'), may hold values from -6 to 6
Outputs:
- grad_inputs: bfloat16 [8, 4096, 2048], P('dp', 'seq')
- grad_weight: float32 [4096, 256], P(('dp', 'seq'))
Inputs may be any that keep to these rules, and one draw needn't show every extreme that they name: `log_decay`: every entry is negative.
All inputs are finite; a program needn't handle non-finite values.
Results may differ from a plain program's by a relative error of at most 0.0069.
Values sent between devices are 32-bit elements; how exact they have to be, the bound alone decides.
A program may use at most 192 MiB of HBM per device.

v0:
```python
import jax
import jax.numpy as jnp
from jax import lax
from jax.sharding import PartitionSpec as P

SHARD_CHANNELS = 32
HEAD_DIM = 64
STATE = 128
SPAN = 128


def span_inputs(proj, inputs, grad_out, step_size, log_decay):
    length = inputs.shape[0]
    spans = length // SPAN
    b_cols = proj[:, :STATE].reshape(spans, SPAN, STATE)
    c_cols = proj[:, STATE:].reshape(spans, SPAN, STATE)
    inputs_c = inputs.reshape(spans, SPAN, SHARD_CHANNELS, HEAD_DIM)
    grad_rows = grad_out.reshape(spans, SPAN, SHARD_CHANNELS, HEAD_DIM)
    step_rows = step_size.reshape(SHARD_CHANNELS, spans, SPAN).transpose(1, 0, 2)
    decay_sum = jnp.cumsum(
        log_decay.reshape(SHARD_CHANNELS, spans, SPAN).transpose(1, 0, 2), axis=2
    )
    span_total = decay_sum[:, :, -1]
    to_end = jnp.exp(span_total[:, :, None] - decay_sum)
    weighted = (
        inputs_c.astype(jnp.float32) * jnp.transpose(step_rows * to_end, (0, 2, 1))[..., None]
    ).astype(jnp.bfloat16)
    scaled = (
        grad_rows.astype(jnp.float32) * jnp.transpose(jnp.exp(decay_sum), (0, 2, 1))[..., None]
    ).astype(jnp.bfloat16)
    own_state = jnp.einsum("cqhp,cqn->chpn", weighted, b_cols, preferred_element_type=jnp.float32)
    own_grad = jnp.einsum("cqhp,cqn->chpn", scaled, c_cols, preferred_element_type=jnp.float32)
    return (
        b_cols,
        c_cols,
        inputs_c,
        grad_rows,
        step_rows,
        decay_sum,
        span_total,
        weighted,
        scaled,
        own_state,
        own_grad,
    )


def span_grads(
    b_cols,
    c_cols,
    inputs_c,
    grad_rows,
    step_rows,
    decay_sum,
    span_total,
    weighted,
    scaled,
    start,
    after,
    skip_gain,
):
    start_bf = start.astype(jnp.bfloat16)
    after_bf = after.astype(jnp.bfloat16)
    row_ids = lax.broadcasted_iota(jnp.int32, (SPAN, SPAN), 0)
    col_ids = lax.broadcasted_iota(jnp.int32, (SPAN, SPAN), 1)
    causal = row_ids >= col_ids
    log_gap = decay_sum[:, :, None] - decay_sum[:, None, :]
    decay_mat = jnp.exp(jnp.where(causal[None], log_gap, -jnp.inf))
    kernel = jnp.dot(c_cols, b_cols.T, preferred_element_type=jnp.float32)
    weights = (decay_mat * kernel[None]).astype(jnp.bfloat16)
    within = jnp.einsum("hsj,shp->jhp", weights, grad_rows, preferred_element_type=jnp.float32)
    carried = jnp.einsum("hpn,jn->jhp", after_bf, b_cols, preferred_element_type=jnp.float32)
    to_end = jnp.exp(span_total[:, None] - decay_sum)
    grad_x = step_rows.T[:, :, None] * (within + to_end.T[:, :, None] * carried) + skip_gain[
        None, :, None
    ] * grad_rows.astype(jnp.float32)
    intersection = jnp.einsum(
        "shp,jhp->hsj", grad_rows, inputs_c, preferred_element_type=jnp.float32
    )
    mixing = jnp.sum(decay_mat * step_rows[:, None, :] * intersection, axis=0).astype(jnp.bfloat16)
    grad_c = jnp.dot(mixing, b_cols, preferred_element_type=jnp.float32) + jnp.dot(
        scaled.reshape(SPAN, -1), start_bf.reshape(-1, STATE), preferred_element_type=jnp.float32
    )
    grad_b = jnp.dot(mixing.T, c_cols, preferred_element_type=jnp.float32) + jnp.dot(
        weighted.reshape(SPAN, -1), after_bf.reshape(-1, STATE), preferred_element_type=jnp.float32
    )
    grad_proj = jnp.concatenate([grad_b, grad_c], axis=1).astype(jnp.bfloat16)
    return (grad_x.astype(jnp.bfloat16).reshape(SPAN, -1), grad_proj)


def exchange(own_state, own_grad, device_total):
    count = lax.axis_size("seq")
    heads, rows, cols = own_state.shape
    marks = jnp.broadcast_to(device_total[:, None, None], (heads, 8, cols))
    payload = jnp.stack(
        [jnp.concatenate([own_state, marks], axis=1), jnp.concatenate([own_grad, marks], axis=1)]
    )
    mine = lax.all_to_all(payload, "seq", 1, 1, tiled=True)
    totals = mine[0, :, rows, 0]
    ends = mine[:, :, :rows, :].reshape(2, count, rows * cols)
    ids = jnp.arange(count)
    target, source, between = (ids[:, None, None], ids[None, :, None], ids[None, None, :])
    fwd_span = (source < between) & (between < target)
    bwd_span = (target < between) & (between < source)
    fwd_log = jnp.sum(jnp.where(fwd_span, totals[None, None, :], 0.0), axis=2)
    bwd_log = jnp.sum(jnp.where(bwd_span, totals[None, None, :], 0.0), axis=2)
    fwd_w = jnp.where(ids[None, :] < ids[:, None], jnp.exp(fwd_log), 0.0)
    bwd_w = jnp.where(ids[None, :] > ids[:, None], jnp.exp(bwd_log), 0.0)
    weights = jnp.stack([fwd_w, bwd_w])
    entries = jnp.einsum(
        "ktj,kjx->ktx",
        weights,
        ends,
        precision=lax.Precision.HIGHEST,
        preferred_element_type=jnp.float32,
    ).reshape(2, count, rows, cols)
    back = lax.all_to_all(entries, "seq", 1, 1, tiled=True)
    return (back[0], back[1])


def scatter_rows(term):
    dp, seq = (lax.axis_size("dp"), lax.axis_size("seq"))
    rows, cols = term.shape
    part = lax.all_to_all(term.reshape(dp, rows // dp, cols), "dp", 0, 0, tiled=True).sum(0)
    part = lax.all_to_all(part.reshape(seq, rows // dp // seq, cols), "seq", 0, 0, tiled=True)
    return part.sum(0)


def on_device(layer_input, proj_weight, inputs, step_size, log_decay, skip_gain, grad_out):
    tokens = layer_input[0]
    length = tokens.shape[0]
    proj = jnp.dot(tokens, proj_weight, preferred_element_type=jnp.float32).astype(jnp.bfloat16)
    pieces = span_inputs(proj, inputs[0], grad_out[0], step_size[0], log_decay[0])
    own_state, own_grad, span_total = (pieces[9], pieces[10], pieces[6])
    empty_state = jnp.zeros((SHARD_CHANNELS, HEAD_DIM, STATE), jnp.float32)

    def advance(state_carry, piece):
        return (jnp.exp(piece[1])[:, None, None] * state_carry + piece[0], state_carry)

    last_state, local_starts = lax.scan(advance, empty_state, (own_state, span_total))
    last_grad, local_afters = lax.scan(advance, empty_state, (own_grad, span_total), reverse=True)
    state_entry, grad_entry = exchange(last_state, last_grad, jnp.sum(span_total, axis=0))
    running = jnp.cumsum(span_total, axis=0)
    before = running - span_total
    behind = jnp.sum(span_total, axis=0)[None] - running
    starts = local_starts + jnp.exp(before)[:, :, None, None] * state_entry[None]
    afters = local_afters + jnp.exp(behind)[:, :, None, None] * grad_entry[None]

    def finish(parts):
        return span_grads(*parts, skip_gain)

    grad_x, grad_proj = lax.map(finish, pieces[:9] + (starts, afters))
    grad_proj = grad_proj.reshape(length, 2 * STATE)
    scale_factor = 1.0 / (length * lax.axis_size("seq"))
    term = jnp.einsum("ld,ln->dn", tokens, grad_proj, preferred_element_type=jnp.float32)
    grad_weight = scatter_rows(term) * scale_factor
    return (grad_x, grad_weight)


def solution(mesh):
    return jax.shard_map(
        on_device,
        mesh=mesh,
        in_specs=(
            P("dp", "seq", None),
            P(),
            P("dp", "seq", None),
            P("dp", None, "seq"),
            P("dp", None, "seq"),
            P(),
            P("dp", "seq", None),
        ),
        out_specs=(P("dp", "seq", None), P(("dp", "seq"), None)),
        check_vma=False,
    )
```

profile of v0, /device:TPU:32, one launch (start us, length us, event | category | flops | bytes accessed | tf_op | source)
XLA Modules:
  0.0 235.9 jit_solution(15632578017909510652)
XLA Ops:
  0.6 0.0 copy-start
  0.6 1.1 reduce_window_sum.17
  1.8 0.2 slice_reduce_fusion.1
  2.0 0.8 multiply_bitcast_fusion
  2.8 1.3 copy.43
  4.1 1.3 copy.42
  5.4 0.0 copy-done
  5.4 1.7 convolution_convert_fusion
  7.1 0.2 fusion.13
  7.3 0.3 convolution_add_fusion.1
  7.6 0.3 convolution_add_fusion
  7.9 0.1 broadcast_in_dim.100
  8.0 0.2 fusion.6
  8.2 0.2 pad_maximum_fusion
  8.4 1.6 copy.45
  9.9 11.4 %all-to-all-start = ((f32[2,32,72,128]{3,2,0,1:T(8,128)}), f32[2,32,72,128]{3,2,0,1:T(8,128)}, u32[]{:S(2)}, u32[]{:S(2)}) async-start(f32[2,32,72,128]{3,2,0,1:T(8,128)} %copy.45), calls=%async_computation | async-start | bytes 4718592 | tf_op jit(solution)/shard_map/all_to_all | solution.py:98
  21.4 55.3 %all-to-all-done = f32[2,32,72,128]{3,2,0,1:T(8,128)} async-done(((f32[2,32,72,128]{3,2,0,1:T(8,128)}), f32[2,32,72,128]{3,2,0,1:T(8,128)}, u32[]{:S(2)}, u32[]{:S(2)}) %all-to-all-start) | async-done | bytes 2359328 | tf_op jit(solution)/shard_map/all_to_all | solution.py:98
  76.7 3.2 %slice.32 = f32[2,32,64,128]{3,2,0,1:T(8,128)} slice(f32[2,32,72,128]{3,2,0,1:T(8,128)} %all-to-all-done), slice={[0:2], [0:32], [0:64], [0:128]} | slice | bytes 4194304 | tf_op jit(solution)/shard_map/slice | solution.py:100
  79.9 3.4 %reshape.335 = f32[2,32,8192]{2,0,1:T(2,128)} reshape(f32[2,32,64,128]{3,2,0,1:T(8,128)} %slice.32) | data formatting | bytes 4194304 | tf_op jit(solution)/shard_map/reshape | solution.py:100
  83.3 1.2 slice_reduce_fusion
  84.5 0.3 select_reduce_fusion.1
  84.9 4.5 %fusion = f32[2,32,8192]{2,1,0:T(8,128)S(1)} fusion(f32[2,32,8192]{2,0,1:T(2,128)} %reshape.335, f32[1,32,32]{2,1,0:T(8,128)S(1)} %bitcast_select_fusion, f32[1,32,32]{2,1,0:T(8,128)S(1)} %bitcast_select_fusion.1), kind=kOutput, calls=%fused_computation.2 | convolution fusion | flops 201328640 | bytes 4202496 | tf_op jit(solution)/shard_map/ktj,kjx->ktx/dot_general | solution.py:110
  89.4 0.4 copy.56
  89.8 1.4 copy.47
  91.3 0.0 copy-start.4
  91.3 6.6 %all-to-all-start.1 = ((f32[2,32,64,128]{3,2,0,1:T(8,128)}), f32[2,32,64,128]{3,2,0,1:T(8,128)}, u32[]{:S(2)}, u32[]{:S(2)}) async-start(f32[2,32,64,128]{3,2,0,1:T(8,128)} %copy.47), calls=%async_computation.1 | async-start | bytes 4194304 | tf_op jit(solution)/shard_map/all_to_all | solution.py:117
  97.9 0.0 copy-done.4
  97.9 1.1 multiply_reduce_fusion
  99.1 0.2 fusion.39
  99.3 0.2 fusion.33
  99.5 1.3 fusion.10
  100.8 45.9 %all-to-all-done.1 = f32[2,32,64,128]{3,2,0,1:T(8,128)} async-done(((f32[2,32,64,128]{3,2,0,1:T(8,128)}), f32[2,32,64,128]{3,2,0,1:T(8,128)}, u32[]{:S(2)}, u32[]{:S(2)}) %all-to-all-start.1) | async-done | bytes 2097184 | tf_op jit(solution)/shard_map/all_to_all | solution.py:117
  146.7 0.0 copy-start.3
  146.7 0.0 copy-start.2
  146.7 0.0 copy-start.1
  146.7 1.9 fusion.11
  148.6 0.0 copy-done.3
  148.6 0.3 fusion.9
  149.0 0.0 copy-done.2
  149.0 0.4 fusion.8
  149.4 0.0 copy-done.1
  149.4 0.7 fusion.15
  150.1 0.6 copy.60
  150.7 54.5 %all_to_all.20 = f32[8,512,256]{1,2,0:T(8,128)} all-to-all(f32[8,512,256]{1,2,0:T(8,128)S(1)} %bitcast.93), channel_id=1, replica_groups=mesh['dp'=8,'seq'=32] {'dp'}, dimensions={0} | all-to-all | bytes 8388608 | tf_op jit(solution)/shard_map/all_to_all | solution.py:124
  205.2 3.5 %reduce_sum.57 = f32[512,256]{0,1:T(8,128)} reduce(f32[8,512,256]{1,2,0:T(8,128)} %all_to_all.20, f32[]{:T(128)} %constant.57.clone.1), dimensions={0}, to_apply=%region_4.5 | reduce | flops 917504 | bytes 4718596 | tf_op jit(solution)/shard_map/reduce_sum | solution.py:124
  208.7 0.0 copy-start.5
  208.7 2.1 copy.51
  210.8 6.5 %all-to-all-start.3 = ((f32[32,16,256]{2,1,0:T(8,128)}), f32[32,16,256]{2,1,0:T(8,128)}, u32[]{:S(2)}, u32[]{:S(2)}) async-start(f32[32,16,256]{2,1,0:T(8,128)} %bitcast.102), calls=%async_computation.3 | async-start | bytes 1048576 | tf_op jit(solution)/shard_map/all_to_all | solution.py:125
  217.3 0.1 exponential_bitcast_fusion.1
  217.4 0.1 fusion.36
  217.5 0.3 convolution_multiply_fusion
  217.8 0.0 copy-done.5
  217.8 1.2 fusion.5
  219.0 1.0 copy.52
  220.0 14.2 %all-to-all-done.3 = f32[32,16,256]{2,1,0:T(8,128)} async-done(((f32[32,16,256]{2,1,0:T(8,128)}), f32[32,16,256]{2,1,0:T(8,128)}, u32[]{:S(2)}, u32[]{:S(2)}) %all-to-all-start.3) | async-done | bytes 524320 | tf_op jit(solution)/shard_map/all_to_all | solution.py:125
  234.2 1.1 reduce_sum.58
  235.3 0.6 broadcast_multiply_fusion
  (5 shorter events, 0.1 us)
Async XLA Ops:
  0.6 4.8 %copy-start = (bf16[4096,256]{1,0:T(8,128)(2,1)S(1)}, bf16[4096,256]{1,0:T(8,128)(2,1)}, u32[]{:S(2)}) copy-start(bf16[4096,256]{1,0:T(8,128)(2,1)} %param.8) | copy-start | bytes 6291460
  9.9 66.7 %all-to-all-start = ((f32[2,32,72,128]{3,2,0,1:T(8,128)}), f32[2,32,72,128]{3,2,0,1:T(8,128)}, u32[]{:S(2)}, u32[]{:S(2)}) async-start(f32[2,32,72,128]{3,2,0,1:T(8,128)} %copy.45), calls=%async_computation | async-start | bytes 4718592 | tf_op jit(solution)/shard_map/all_to_all | solution.py:98
  91.3 6.7 %copy-start.4 = (f32[1,32,128]{2,1,0:T(8,128)S(1)}, f32[1,32,128]{2,1,0:T(8,128)}, u32[]{:S(2)}) copy-start(f32[1,32,128]{2,1,0:T(8,128)} %param.10) | copy-start | bytes 49156
  91.3 55.4 %all-to-all-start.1 = ((f32[2,32,64,128]{3,2,0,1:T(8,128)}), f32[2,32,64,128]{3,2,0,1:T(8,128)}, u32[]{:S(2)}, u32[]{:S(2)}) async-start(f32[2,32,64,128]{3,2,0,1:T(8,128)} %copy.47), calls=%async_computation.1 | async-start | bytes 4194304 | tf_op jit(solution)/shard_map/all_to_all | solution.py:117
  146.7 1.9 copy-start.3
  146.7 2.3 copy-start.2
  146.7 2.7 %copy-start.1 = (bf16[1,128,4096]{2,1,0:T(8,128)(2,1)S(1)}, bf16[1,128,4096]{2,1,0:T(8,128)(2,1)}, u32[]{:S(2)}) copy-start(bf16[1,128,4096]{2,1,0:T(8,128)(2,1)} %param.7) | copy-start | bytes 3145732
  208.7 9.1 %copy-start.5 = (f32[32]{0:T(128)S(1)}, f32[32]{0:T(128)}, u32[]{:S(2)}) copy-start(f32[32]{0:T(128)} %param.12) | copy-start | bytes 388
  210.8 23.4 %all-to-all-start.3 = ((f32[32,16,256]{2,1,0:T(8,128)}), f32[32,16,256]{2,1,0:T(8,128)}, u32[]{:S(2)}, u32[]{:S(2)}) async-start(f32[32,16,256]{2,1,0:T(8,128)} %bitcast.102), calls=%async_computation.3 | async-start | bytes 1048576 | tf_op jit(solution)/shard_map/all_to_all | solution.py:125
where the time goes:
time: 237 us; the launch traced here: 236 us
  waiting for transfers between devices  115 us (49%)
  blocking collectives  54.5 us (23%)
  starting transfers between devices  24.6 us (10%)
  local copies, waits for them, and re-layouts  17.8 us (8%)
  other arithmetic  11.4 us (5%)
  matrix products  11.3 us (5%)
    all_to_all x1, waiting for transfers between devices, exchange(): mine = lax.all_to_all(payload, 'seq', 1, 1, tiled=True)  55.3 us
    all_to_all x1, blocking collectives, scatter_rows(): lax.all_to_all(term.reshape(dp, rows // dp, cols), 'dp', 0, 0, tiled=True)  54.5 us
    all_to_all x1, waiting for transfers between devices, exchange(): back = lax.all_to_all(entries, 'seq', 1, 1, tiled=True)  45.9 us
    all_to_all x1, waiting for transfers between devices, scatter_rows(): lax.all_to_all(part.reshape(seq, rows // dp // seq, cols), 'seq', 0, 0, t...  14.2 us
    all_to_all x1, starting transfers between devices, exchange(): mine = lax.all_to_all(payload, 'seq', 1, 1, tiled=True)  11.4 us
    all_to_all x1, starting transfers between devices, exchange(): back = lax.all_to_all(entries, 'seq', 1, 1, tiled=True)  6.64 us
    all_to_all x1, starting transfers between devices, scatter_rows(): lax.all_to_all(part.reshape(seq, rows // dp // seq, cols), 'seq', 0, 0, t...  6.52 us
  transfers between devices with their start and end apart: 3, of which 3 were waited for; matrix products, arithmetic and copies ran while one was open for 2% of the time, Pallas kernels for 0%

commit v1 on v0

--- a/solution.py
+++ b/solution.py
@@ -7,6 +7,12 @@
 HEAD_DIM = 64
 STATE = 128
 SPAN = 128
+
+
+def swap_blocks(value, axis, split, join):
+    pieces = jnp.split(value, lax.axis_size(axis), axis=split)
+    arrived = lax.all_to_all(jnp.stack(pieces), axis, 0, 0)
+    return jnp.concatenate(arrived, axis=join)
 
 
 def span_inputs(proj, inputs, grad_out, step_size, log_decay):
@@ -114,7 +120,7 @@
         precision=lax.Precision.HIGHEST,
         preferred_element_type=jnp.float32,
     ).reshape(2, count, rows, cols)
-    back = lax.all_to_all(entries, "seq", 1, 1, tiled=True)
+    back = swap_blocks(entries, "seq", 1, 1)
     return (back[0], back[1])
 
 

time: 237 us -> 252 us (1.063)
  local copies, waits for them, and re-layouts: 17.8 us -> 36.3 us
  waiting for transfers between devices: 115 us -> 112 us
    unnamed x16 -> x47, local copies, waits for them, and re-layouts: 4.04 us -> 24.4 us
    all_to_all x1, waiting for transfers between devices: 14.2 us -> 11.1 us  [scatter_rows(): lax.all_to_all(part.reshape(seq, rows // dp // seq, cols), 'seq', 0, 0, t...]
  transfers between devices with their start and end apart: 3 -> 3, of which waited for: 3 -> 3; matrix products, arithmetic and copies ran while one was open for 2% -> 3% of each run, Pallas kernels for 0% -> 0%
where the time goes in v1:
time: 252 us; the launch traced here: 251 us
  waiting for transfers between devices  112 us (44%)
  blocking collectives  54.5 us (22%)
  local copies, waits for them, and re-layouts  36.3 us (14%)
  starting transfers between devices  24.5 us (10%)
  matrix products  13.3 us (5%)
  other arithmetic  9.55 us (4%)
    all_to_all x1, waiting for transfers between devices, exchange(): mine = lax.all_to_all(payload, 'seq', 1, 1, tiled=True)  55.3 us
    all_to_all x1, blocking collectives, scatter_rows(): lax.all_to_all(term.reshape(dp, rows // dp, cols), 'dp', 0, 0, tiled=True)  54.5 us
    all_to_all x1, waiting for transfers between devices, swap_blocks(): arrived = lax.all_to_all(jnp.stack(pieces), axis, 0, 0)  45.9 us
    unnamed x47, local copies, waits for them, and re-layouts  24.4 us
    all_to_all x1, starting transfers between devices, exchange(): mine = lax.all_to_all(payload, 'seq', 1, 1, tiled=True)  11.4 us
    all_to_all x1, waiting for transfers between devices, scatter_rows(): lax.all_to_all(part.reshape(seq, rows // dp // seq, cols), 'seq', 0, 0, t...  11.1 us
    all_to_all x1, starting transfers between devices, swap_blocks(): arrived = lax.all_to_all(jnp.stack(pieces), axis, 0, 0)  6.64 us
    all_to_all x1, starting transfers between devices, scatter_rows(): lax.all_to_all(part.reshape(seq, rows // dp // seq, cols), 'seq', 0, 0, t...  6.46 us
  transfers between devices with their start and end apart: 3, of which 3 were waited for; matrix products, arithmetic and copies ran while one was open for 3% of the time, Pallas kernels for 0%

profile of v1, /device:TPU:32, one launch (start us, length us, event | category | flops | bytes accessed | tf_op | source)
XLA Modules:
  0.0 251.4 jit_solution(4525466821424008442)
XLA Ops:
  0.6 1.1 reduce_window_sum.17
  2.0 0.8 multiply_bitcast_fusion
  2.8 1.3 copy.169
  4.1 1.3 copy.168
  5.4 1.7 convolution_convert_fusion
  8.4 1.6 copy.171
  9.9 11.4 %all-to-all-start = ((f32[2,32,72,128]{3,2,0,1:T(8,128)}), f32[2,32,72,128]{3,2,0,1:T(8,128)}, u32[]{:S(2)}, u32[]{:S(2)}) async-start(f32[2,32,72,128]{3,2,0,1:T(8,128)} %copy.171), calls=%async_computation | async-start | bytes 4718592 | tf_op jit(solution)/shard_map/all_to_all | solution.py:104
  21.4 55.3 %all-to-all-done = f32[2,32,72,128]{3,2,0,1:T(8,128)} async-done(((f32[2,32,72,128]{3,2,0,1:T(8,128)}), f32[2,32,72,128]{3,2,0,1:T(8,128)}, u32[]{:S(2)}, u32[]{:S(2)}) %all-to-all-start) | async-done | bytes 2359328 | tf_op jit(solution)/shard_map/all_to_all | solution.py:104
  76.7 3.2 %slice.37 = f32[2,32,64,128]{3,2,0,1:T(8,128)} slice(f32[2,32,72,128]{3,2,0,1:T(8,128)} %all-to-all-done), slice={[0:2], [0:32], [0:64], [0:128]} | slice | bytes 4194304 | tf_op jit(solution)/shard_map/slice | solution.py:106
  79.9 3.4 %reshape.361 = f32[2,32,8192]{2,0,1:T(2,128)} reshape(f32[2,32,64,128]{3,2,0,1:T(8,128)} %slice.37) | data formatting | bytes 4194304 | tf_op jit(solution)/shard_map/reshape | solution.py:106
  83.3 1.2 slice_reduce_fusion
  84.5 0.3 select_reduce_fusion.1
  84.9 4.5 %fusion = f32[2,32,8192]{2,1,0:T(8,128)S(1)} fusion(f32[2,32,8192]{2,0,1:T(2,128)} %reshape.361, f32[1,32,32]{2,1,0:T(8,128)S(1)} %bitcast_select_fusion, f32[1,32,32]{2,1,0:T(8,128)S(1)} %bitcast_select_fusion.1), kind=kOutput, calls=%fused_computation.2 | convolution fusion | flops 201328640 | bytes 4202496 | tf_op jit(solution)/shard_map/ktj,kjx->ktx/dot_general | solution.py:116
  89.4 0.4 copy.245
  89.8 0.6 constant_dynamic-update-slice_fusion.31
  90.5 0.6 constant_dynamic-update-slice_fusion.30
  91.1 0.6 constant_dynamic-update-slice_fusion.29
  91.7 0.6 constant_dynamic-update-slice_fusion.28
  92.3 0.6 constant_dynamic-update-slice_fusion.27
  92.9 0.6 constant_dynamic-update-slice_fusion.26
  93.6 0.6 constant_dynamic-update-slice_fusion.25
  94.2 0.6 constant_dynamic-update-slice_fusion.24
  94.8 0.6 constant_dynamic-update-slice_fusion.23
  95.4 0.6 constant_dynamic-update-slice_fusion.22
  96.1 0.6 constant_dynamic-update-slice_fusion.21
  96.7 0.6 constant_dynamic-update-slice_fusion.20
  97.3 0.6 constant_dynamic-update-slice_fusion.19
  97.9 0.6 constant_dynamic-update-slice_fusion.18
  98.6 0.6 constant_dynamic-update-slice_fusion.17
  99.2 0.6 constant_dynamic-update-slice_fusion.16
  99.8 0.6 constant_dynamic-update-slice_fusion.15
  100.4 0.6 constant_dynamic-update-slice_fusion.14
  101.1 0.6 constant_dynamic-update-slice_fusion.13
  101.7 0.6 constant_dynamic-update-slice_fusion.12
  102.3 0.6 constant_dynamic-update-slice_fusion.11
  102.9 0.6 constant_dynamic-update-slice_fusion.10
  103.5 0.6 constant_dynamic-update-slice_fusion.9
  104.2 0.6 constant_dynamic-update-slice_fusion.8
  104.8 0.6 constant_dynamic-update-slice_fusion.7
  105.4 0.6 constant_dynamic-update-slice_fusion.6
  106.0 0.6 constant_dynamic-update-slice_fusion.5
  106.7 0.6 constant_dynamic-update-slice_fusion.4
  107.3 0.6 constant_dynamic-update-slice_fusion.3
  107.9 0.6 constant_dynamic-update-slice_fusion.2
  108.5 0.6 constant_dynamic-update-slice_fusion.1
  109.1 0.6 constant_dynamic-update-slice_fusion
  109.8 6.6 %all-to-all-start.1 = ((f32[32,2,1,64,128]{4,3,2,1,0:T(8,128)}), f32[32,2,1,64,128]{4,3,2,1,0:T(8,128)}, u32[]{:S(2)}, u32[]{:S(2)}) async-start(f32[32,2,1,64,128]{4,3,2,1,0:T(8,128)} %constant_dynamic-update-slice_fusion), calls=%async_computation.1 | async-start | bytes 4194304 | tf_op jit(solution)/shard_map/all_to_all | solution.py:14
  116.5 1.1 multiply_reduce_fusion
  118.0 1.3 fusion.10
  119.3 45.9 %all-to-all-done.1 = f32[32,2,1,64,128]{4,3,2,1,0:T(8,128)} async-done(((f32[32,2,1,64,128]{4,3,2,1,0:T(8,128)}), f32[32,2,1,64,128]{4,3,2,1,0:T(8,128)}, u32[]{:S(2)}, u32[]{:S(2)}) %all-to-all-start.1) | async-done | bytes 2097184 | tf_op jit(solution)/shard_map/all_to_all | solution.py:14
  165.2 1.9 multiply_convert_fusion.2
  167.1 0.4 fusion.8
  167.5 0.4 fusion.9
  167.9 0.7 fusion.15
  168.6 0.6 copy.249
  169.2 54.5 %all_to_all.20 = f32[8,512,256]{1,2,0:T(8,128)} all-to-all(f32[8,512,256]{1,2,0:T(8,128)S(1)} %bitcast.288), channel_id=1, replica_groups=mesh['dp'=8,'seq'=32] {'dp'}, dimensions={0} | all-to-all | bytes 8388608 | tf_op jit(solution)/shard_map/all_to_all | solution.py:130
  223.7 2.7 %reduce_sum.57 = f32[512,256]{0,1:T(8,128)S(1)} reduce(f32[8,512,256]{1,2,0:T(8,128)} %all_to_all.20, f32[]{:T(128)} %constant.57.clone.1), dimensions={0}, to_apply=%region_4.5 | reduce | flops 917504 | bytes 4718596 | tf_op jit(solution)/shard_map/reduce_sum | solution.py:130
  226.4 1.0 copy.208
  227.4 6.5 %all-to-all-start.3 = ((f32[32,16,256]{2,1,0:T(8,128)}), f32[32,16,256]{2,1,0:T(8,128)S(1)}, u32[]{:S(2)}, u32[]{:S(2)}) async-start(f32[32,16,256]{2,1,0:T(8,128)} %bitcast.327), calls=%async_computation.3 | async-start | bytes 1048576 | tf_op jit(solution)/shard_map/all_to_all | solution.py:131
  234.1 1.6 convolution_multiply_fusion
  235.7 1.9 fusion.5
  237.6 2.0 copy.209
  239.6 11.1 %all-to-all-done.3 = f32[32,16,256]{2,1,0:T(8,128)S(1)} async-done(((f32[32,16,256]{2,1,0:T(8,128)}), f32[32,16,256]{2,1,0:T(8,128)S(1)}, u32[]{:S(2)}, u32[]{:S(2)}) %all-to-all-start.3) | async-done | bytes 524320 | tf_op jit(solution)/shard_map/all_to_all | solution.py:131
  250.8 0.6 broadcast_multiply_fusion
  (29 shorter events, 2.1 us)
Async XLA Ops:
  0.6 4.8 %copy-start = (bf16[4096,256]{1,0:T(8,128)(2,1)S(1)}, bf16[4096,256]{1,0:T(8,128)(2,1)}, u32[]{:S(2)}) copy-start(bf16[4096,256]{1,0:T(8,128)(2,1)} %param.8) | copy-start | bytes 6291460
  9.9 66.7 %all-to-all-start = ((f32[2,32,72,128]{3,2,0,1:T(8,128)}), f32[2,32,72,128]{3,2,0,1:T(8,128)}, u32[]{:S(2)}, u32[]{:S(2)}) async-start(f32[2,32,72,128]{3,2,0,1:T(8,128)} %copy.171), calls=%async_computation | async-start | bytes 4718592 | tf_op jit(solution)/shard_map/all_to_all | solution.py:104
  109.8 6.7 %copy-start.4 = (f32[1,32,128]{2,1,0:T(8,128)S(1)}, f32[1,32,128]{2,1,0:T(8,128)}, u32[]{:S(2)}) copy-start(f32[1,32,128]{2,1,0:T(8,128)} %param.10) | copy-start | bytes 49156
  109.8 55.4 %all-to-all-start.1 = ((f32[32,2,1,64,128]{4,3,2,1,0:T(8,128)}), f32[32,2,1,64,128]{4,3,2,1,0:T(8,128)}, u32[]{:S(2)}, u32[]{:S(2)}) async-start(f32[32,2,1,64,128]{4,3,2,1,0:T(8,128)} %constant_dynamic-update-slice_fusion), calls=%async_computation.1 | async-start | bytes 4194304 | tf_op jit(solution)/shard_map/all_to_all | solution.py:14
  119.3 47.8 %copy-start.3 = (bf16[128,32,64]{0,2,1:T(8,128)(2,1)S(1)}, bf16[128,32,64]{0,2,1:T(8,128)(2,1)}, u32[]{:S(2)}) copy-start(bf16[128,32,64]{0,2,1:T(8,128)(2,1)} %get-tuple-element.83) | copy-start | bytes 1572868
  165.2 2.3 copy-start.2
  165.2 2.6 %copy-start.1 = (bf16[1,128,4096]{2,1,0:T(8,128)(2,1)S(1)}, bf16[1,128,4096]{2,1,0:T(8,128)(2,1)}, u32[]{:S(2)}) copy-start(bf16[1,128,4096]{2,1,0:T(8,128)(2,1)} %param.7) | copy-start | bytes 3145732
  226.4 9.3 %copy-start.5 = (f32[32]{0:T(128)S(1)}, f32[32]{0:T(128)}, u32[]{:S(2)}) copy-start(f32[32]{0:T(128)} %param.12) | copy-start | bytes 388
  227.4 23.3 %all-to-all-start.3 = ((f32[32,16,256]{2,1,0:T(8,128)}), f32[32,16,256]{2,1,0:T(8,128)S(1)}, u32[]{:S(2)}, u32[]{:S(2)}) async-start(f32[32,16,256]{2,1,0:T(8,128)} %bitcast.327), calls=%async_computation.3 | async-start | bytes 1048576 | tf_op jit(solution)/shard_map/all_to_all | solution.py:131
